TPU v7x, 32 devices: a whole 2x2x4 slice. The times are simulated.
32 devices in a mesh: pairs: 2 (over y), ctx: 8 (over z, x), head: 2 (over core).
Axes of the slice: x: 2, y: 2, z: 4, core: 2. Of those that a mesh axis runs over, the one named last changes fastest.
Arguments:
- hidden: bfloat16 [16, 2, 8192], P(('pairs', 'ctx')), parts along dimension 0, may hold values from -6 to 6
- wq: bfloat16 [8192, 4096], P('ctx', 'head'), may hold values from -0.0625 to 0.0625
- wkv: bfloat16 [2, 8192, 512], P(None, 'ctx', 'head'), may hold values from -0.0625 to 0.0625
- bias_q: bfloat16 [4096], P('head'), may hold values from -5.2 to 5.2
- bias_kv: bfloat16 [2, 512], P(None, 'head'), may hold values from -5.2 to 5.2
- key_value_cache: bfloat16 [2, 8192, 512], P(None, ('pairs', 'ctx'), 'head'), parts along dimension 1, may hold values from -46 to 46, as said below
- prompt_len: int32 [2], P('pairs'), parts along dimension 0, may hold values from 512 to 4096
- resp_len: int32 [4], P('pairs'), parts along dimension 0, may hold values from 2 to 8
Outputs:
- attn_out: bfloat16 [16, 2, 4096], P(('pairs', 'ctx'), None, 'head'), parts along dimension 0
There are 2 independent parts, one for each index of `pairs`. A program takes and returns all parts, laid end to end along the dimension named above; an argument that names none is the same for every part. Nothing has to cross between parts.
Inputs may be any that keep to these rules, and one draw needn't show every extreme that they name: `key_value_cache`: entries beyond prompt_len are padding and must not be attended to. Prompt positions from prompt_len on are padding. Token slots of response r from resp_len[r] on are padding.
All inputs are finite; a program needn't handle non-finite values.
Results may differ from a plain program's by a relative error of at most 0.025.
Values may be sent and summed in bfloat16 or wider, within the bound.
No kernel may reach another device: no remote copies, remote signals or barrier semaphores. Data moves between devices by JAX's collectives and lax.ppermute only.
A program may use at most 64 MiB of HBM per device.

v0:
```python
import jax
import jax.numpy as jnp
from jax import lax
from jax.sharding import PartitionSpec as P

HEAD_SIZE = 128
NEG_FILL = -1e30


def shards(hidden, wq, wkv, bias_q, bias_kv, key_value_cache, prompt_len, resp_len):
    tok_dev = hidden.shape[0]
    ctx_index = lax.axis_index("ctx")
    resp_tokens = tok_dev * lax.axis_size("ctx")
    q_width = wq.shape[1]
    k_width = wkv.shape[2]
    kv_local = k_width // HEAD_SIZE
    query_group_width = q_width // k_width
    score_scale = HEAD_SIZE ** (-0.5)
    row_count = 2 * tok_dev
    columns = lax.all_to_all(hidden, "ctx", split_axis=2, concat_axis=0, tiled=True)
    flat_rows = columns.reshape(2 * resp_tokens, columns.shape[2])
    weights_all = jnp.concatenate((wq, wkv[0], wkv[1]), axis=1)
    bias_all = jnp.concatenate((bias_q, bias_kv[0], bias_kv[1])).astype(jnp.float32)
    summed = lax.psum(jnp.dot(flat_rows, weights_all, preferred_element_type=jnp.float32), "ctx")
    projected = (summed + bias_all).astype(jnp.bfloat16)
    owned = lax.dynamic_slice_in_dim(projected, ctx_index * row_count, row_count, 0)
    query_rows = projected[:, :q_width].reshape(
        2 * resp_tokens, kv_local, query_group_width, HEAD_SIZE
    )
    cache_len = key_value_cache.shape[1]
    key_block = min(512, cache_len)
    block_count = cache_len // key_block
    prompt_key_rows = key_value_cache[0].reshape(block_count, key_block, kv_local, HEAD_SIZE)
    prompt_value_rows = key_value_cache[1].reshape(block_count, key_block, kv_local, HEAD_SIZE)
    first_slot = ctx_index * cache_len
    live_limit = prompt_len[0]

    def visit(carry, inputs):
        running_max, running_sum, weighted = carry
        block_keys, block_values, block_index = inputs
        scores = (
            jnp.einsum("rgjd,kgd->grjk", query_rows, block_keys, preferred_element_type=jnp.float32)
            * score_scale
        )
        position = first_slot + block_index * key_block + lax.iota(jnp.int32, key_block)
        is_live = position < live_limit
        scores = jnp.where(is_live, scores, NEG_FILL)
        new_max = jnp.maximum(running_max, jnp.max(scores, axis=-1))
        unscaled = jnp.where(is_live, jnp.exp(scores - new_max[..., None]), 0.0)
        factor = jnp.exp(running_max - new_max)
        running_sum = running_sum * factor + jnp.sum(unscaled, axis=-1)
        weighted = weighted * factor[..., None] + jnp.einsum(
            "grjk,kgd->grjd",
            unscaled.astype(jnp.bfloat16),
            block_values,
            preferred_element_type=jnp.float32,
        )
        return ((new_max, running_sum, weighted), None)

    statistic_shape = (kv_local, 2 * resp_tokens, query_group_width)
    start_state = (
        jnp.full(statistic_shape, NEG_FILL, jnp.float32),
        jnp.zeros(statistic_shape, jnp.float32),
        jnp.zeros(statistic_shape + (HEAD_SIZE,), jnp.float32),
    )
    closing_state, unused = lax.scan(
        visit,
        start_state,
        (prompt_key_rows, prompt_value_rows, jnp.arange(block_count, dtype=jnp.int32)),
    )
    owned_q = owned[:, :q_width].reshape(tok_dev, 2, kv_local, query_group_width, HEAD_SIZE)
    fresh_key_rows = projected[:, q_width : q_width + k_width].reshape(
        resp_tokens, 2, kv_local, HEAD_SIZE
    )
    fresh_value_rows = projected[:, q_width + k_width :].reshape(
        resp_tokens, 2, kv_local, HEAD_SIZE
    )
    self_scores = (
        jnp.einsum("trgjd,urgd->gtrju", owned_q, fresh_key_rows, preferred_element_type=jnp.float32)
        * score_scale
    )
    token_pos = ctx_index * tok_dev + lax.iota(jnp.int32, tok_dev)
    key_pos = lax.iota(jnp.int32, resp_tokens)
    self_live = (key_pos[None, None, :] <= token_pos[:, None, None]) & (
        key_pos[None, None, :] < resp_len[None, :, None]
    )
    self_live = self_live[None, :, :, None, :]
    self_scores = jnp.where(self_live, self_scores, NEG_FILL)
    self_max = jnp.max(self_scores, axis=-1)
    self_weights = jnp.where(self_live, jnp.exp(self_scores - self_max[..., None]), 0.0)
    self_sum = jnp.sum(self_weights, axis=-1)
    self_acc = jnp.einsum(
        "gtrju,urgd->gtrjd",
        self_weights.astype(jnp.bfloat16),
        fresh_value_rows,
        preferred_element_type=jnp.float32,
    )
    lead_shape = (1, kv_local, resp_tokens, 2, query_group_width)
    remote_max, remote_sum, remote_acc = (
        lax.all_to_all(
            closing_state[0].reshape(lead_shape), "ctx", split_axis=2, concat_axis=0, tiled=True
        ),
        lax.all_to_all(
            closing_state[1].reshape(lead_shape), "ctx", split_axis=2, concat_axis=0, tiled=True
        ),
        lax.all_to_all(
            closing_state[2].reshape(lead_shape + (HEAD_SIZE,)),
            "ctx",
            split_axis=2,
            concat_axis=0,
            tiled=True,
        ),
    )
    overall = jnp.maximum(jnp.max(remote_max, axis=0), self_max)
    remote_factor = jnp.exp(remote_max - overall[None])
    prompt_acc = jnp.sum(remote_factor[..., None] * remote_acc, axis=0)
    prompt_total = jnp.sum(remote_factor * remote_sum, axis=0)
    self_factor = jnp.exp(self_max - overall)
    numerator = prompt_acc + self_factor[..., None] * self_acc
    denominator = prompt_total + self_factor * self_sum
    result = numerator / denominator[..., None]
    row_live = token_pos[:, None] < resp_len[None, :]
    result = jnp.where(row_live[None, :, :, None, None], result, 0.0)
    return jnp.transpose(result, (1, 2, 0, 3, 4)).reshape(tok_dev, 2, q_width).astype(jnp.bfloat16)


def solution(mesh):
    return jax.shard_map(
        shards,
        mesh=mesh,
        in_specs=(
            P(("pairs", "ctx"), None, None),
            P("ctx", "head"),
            P(None, "ctx", "head"),
            P("head"),
            P(None, "head"),
            P(None, ("pairs", "ctx"), "head"),
            P("pairs"),
            P("pairs"),
        ),
        out_specs=P(("pairs", "ctx"), None, "head"),
        check_vma=False,
    )
```

profile of v0, /device:TPU:0, one launch (start us, length us, event | category | flops | bytes accessed | tf_op | source)
XLA Modules:
  0.0 205.0 jit_solution(12979786244044143791)
XLA Ops:
  6.5 8.2 %copy.38 = bf16[1,2,8192]{1,0,2:T(2,128)(2,1)} copy(bf16[1,2,8192]{2,1,0:T(2,128)(2,1)} %param.8) | data formatting | bytes 65536 | tf_op args[0]
  14.8 0.5 broadcast.132
  15.3 0.0 copy-start
  15.3 45.3 %reduce.10 = bf16[8192,2]{1,0:T(8,128)(2,1)S(1)} reduce(bf16[8192,1,2]{2,1,0:T(2,128)(2,1)} %bitcast.123, bf16[]{:T(256)} %broadcast.132), dimensions={1}, to_apply=%bitcast.111.reduce_sub_computation | reduce | bytes 65538
  60.6 0.0 copy-start.3
  60.6 0.0 copy-start.2
  60.6 3.8 %reshape.289 = bf16[8,2,1024]{2,1,0:T(2,128)(2,1)} reshape(bf16[8192,2]{1,0:T(8,128)(2,1)S(1)} %reduce.10) | data formatting | bytes 65536
  64.4 7.3 %all-to-all-start = ((bf16[8,2,1024]{2,1,0:T(2,128)(2,1)}), bf16[8,2,1024]{2,1,0:T(2,128)(2,1)S(1)}, u32[]{:S(2)}, u32[]{:S(2)}) async-start(bf16[8,2,1024]{2,1,0:T(2,128)(2,1)} %reshape.289), calls=%async_computation | async-start | bytes 65536 | tf_op jit(solution)/shard_map/all_to_all | solution.py:20
  71.7 0.0 all-reduce.2.cloned.1.call-start
  71.8 1.1 fusion.45
  72.8 0.0 copy-done
  72.8 0.1 slice_bitcast_fusion.1
  73.6 0.0 copy-done.3
  73.6 0.1 compare_and_fusion
  73.7 0.0 copy-done.2
  73.7 4.7 %all-to-all-done = bf16[8,2,1024]{2,1,0:T(2,128)(2,1)S(1)} async-done(((bf16[8,2,1024]{2,1,0:T(2,128)(2,1)}), bf16[8,2,1024]{2,1,0:T(2,128)(2,1)S(1)}, u32[]{:S(2)}, u32[]{:S(2)}) %all-to-all-start) | async-done | bytes 32800 | tf_op jit(solution)/shard_map/all_to_all | solution.py:20
  78.4 6.3 %reshape.290 = bf16[8192,1,2]{2,1,0:T(2,128)(2,1)} reshape(bf16[8,2,1024]{2,1,0:T(2,128)(2,1)S(1)} %all-to-all-done) | data formatting | bytes 65536
  84.7 8.1 %copy.39 = bf16[1,2,8192]{2,1,0:T(2,128)(2,1)S(1)} copy(bf16[1,2,8192]{1,0,2:T(2,128)(2,1)} %bitcast.124) | data formatting | bytes 65536 | tf_op jit(solution)/shard_map/all_to_all | solution.py:20
  92.8 0.0 copy-start.1
  92.9 3.3 %fusion.6 = f32[16,2560]{1,0:T(8,128)} fusion(bf16[16,1024]{1,0:T(8,128)(2,1)S(1)} %reshape.278, bf16[1024,256]{1,0:T(8,128)(2,1)S(1)} %get-tuple-element.26, bf16[1024,256]{1,0:T(8,128)(2,1)S(1)} %get-tuple-element.25, bf16[1024,2048]{1,0:T(8,128)(2,1)} %param.9), kind=kOutput, calls=%fused_computation.6 | convolution fusion | flops 99614720 | bytes 5439488 | tf_op jit(solution)/shard_map/dot_general | solution.py:24
  96.2 0.0 all-reduce.2.cloned.1.call-update
  96.2 0.1 copy.62
  96.4 0.1 copy.61
  96.5 0.0 copy-done.1
  96.6 67.2 %all-reduce.2.cloned.1.call-done = f32[16,2560]{1,0:T(8,128)} async-done(((f32[16,2560]{1,0:T(8,128)}), f32[16,2560]{1,0:T(8,128)}) %all-reduce.2.cloned.1.call-update) | async-done | bytes 163856 | tf_op jit(solution)/shard_map/psum | solution.py:24
  163.8 0.9 add_convert_fusion
  164.7 0.3 fusion.47
  165.1 0.6 copy.44
  165.7 4.4 %all-to-all-start.1 = ((f32[1,2,8,2,8]{4,3,1,0,2:T(2,128)}), f32[1,2,8,2,8]{4,3,1,0,2:T(2,128)S(1)}, u32[]{:S(2)}, u32[]{:S(2)}) async-start(f32[1,2,8,2,8]{4,3,1,0,2:T(2,128)} %copy.44), calls=%async_computation.1 | async-start | bytes 32768 | tf_op jit(solution)/shard_map/all_to_all | solution.py:100
  170.1 0.2 fusion.18
  170.4 0.3 convolution_add_fusion
  170.6 0.1 fusion.48
  170.8 0.1 fusion.29
  170.9 0.6 copy.49
  171.5 0.6 copy.52
  172.1 4.5 %all-to-all-done.1 = f32[1,2,8,2,8]{4,3,1,0,2:T(2,128)S(1)} async-done(((f32[1,2,8,2,8]{4,3,1,0,2:T(2,128)}), f32[1,2,8,2,8]{4,3,1,0,2:T(2,128)S(1)}, u32[]{:S(2)}, u32[]{:S(2)}) %all-to-all-start.1) | async-done | bytes 1056 | tf_op jit(solution)/shard_map/all_to_all | solution.py:100
  176.6 3.3 %all-to-all-start.3 = ((f32[1,2,8,2,8]{4,3,1,0,2:T(2,128)}), f32[1,2,8,2,8]{4,3,1,0,2:T(2,128)S(1)}, u32[]{:S(2)}, u32[]{:S(2)}) async-start(f32[1,2,8,2,8]{4,3,1,0,2:T(2,128)} %copy.52), calls=%async_computation.3 | async-start | bytes 32768 | tf_op jit(solution)/shard_map/all_to_all | solution.py:103
  180.0 6.5 %all-to-all-done.3 = f32[1,2,8,2,8]{4,3,1,0,2:T(2,128)S(1)} async-done(((f32[1,2,8,2,8]{4,3,1,0,2:T(2,128)}), f32[1,2,8,2,8]{4,3,1,0,2:T(2,128)S(1)}, u32[]{:S(2)}, u32[]{:S(2)}) %all-to-all-start.3) | async-done | bytes 1056 | tf_op jit(solution)/shard_map/all_to_all | solution.py:103
  186.5 3.4 %all-to-all-start.2 = ((f32[1,2,8,2,8,128]{5,4,3,1,0,2:T(8,128)}), f32[1,2,8,2,8,128]{5,4,3,1,0,2:T(8,128)S(1)}, u32[]{:S(2)}, u32[]{:S(2)}) async-start(f32[1,2,8,2,8,128]{5,4,3,1,0,2:T(8,128)} %copy.49), calls=%async_computation.2 | async-start | bytes 262144 | tf_op jit(solution)/shard_map/all_to_all | solution.py:106
  190.0 7.2 %all-to-all-done.2 = f32[1,2,8,2,8,128]{5,4,3,1,0,2:T(8,128)S(1)} async-done(((f32[1,2,8,2,8,128]{5,4,3,1,0,2:T(8,128)}), f32[1,2,8,2,8,128]{5,4,3,1,0,2:T(8,128)S(1)}, u32[]{:S(2)}, u32[]{:S(2)}) %all-to-all-start.2) | async-done | bytes 131104 | tf_op jit(solution)/shard_map/all_to_all | solution.py:106
  197.2 0.1 fusion.24
  197.3 0.2 fusion.15
  197.5 0.6 convert_element_type.36
  (22 shorter events, 0.3 us)
Async XLA Ops:
  15.3 57.6 %copy-start = (bf16[2,1024,256]{2,1,0:T(8,128)(2,1)S(1)}, bf16[2,1024,256]{2,1,0:T(8,128)(2,1)}, u32[]{:S(2)}) copy-start(bf16[2,1024,256]{2,1,0:T(8,128)(2,1)} %param.10) | copy-start | bytes 3145732
  60.6 13.0 %copy-start.3 = (s32[2]{0:T(128)S(1)}, s32[2]{0:T(128)}, u32[]{:S(2)}) copy-start(s32[2]{0:T(128)} %param.15) | copy-start | bytes 28
  60.6 13.1 %copy-start.2 = (bf16[2,256]{1,0:T(2,128)(2,1)S(1)}, bf16[2,256]{1,0:T(2,128)(2,1)}, u32[]{:S(2)}) copy-start(bf16[2,256]{1,0:T(2,128)(2,1)} %param.12) | copy-start | bytes 3076
  64.4 14.0 %all-to-all-start = ((bf16[8,2,1024]{2,1,0:T(2,128)(2,1)}), bf16[8,2,1024]{2,1,0:T(2,128)(2,1)S(1)}, u32[]{:S(2)}, u32[]{:S(2)}) async-start(bf16[8,2,1024]{2,1,0:T(2,128)(2,1)} %reshape.289), calls=%async_computation | async-start | bytes 65536 | tf_op jit(solution)/shard_map/all_to_all | solution.py:20
  71.7 92.0 %all-reduce.2.cloned.1.call-start = ((), (), s32[]{:S(2)}) async-start(), calls=%async_computation.4 | async-start | bytes 327680 | tf_op jit(solution)/shard_map/psum | solution.py:24
  92.8 3.7 %copy-start.1 = (bf16[2048]{0:T(1024)(128)(2,1)S(1)}, bf16[2048]{0:T(1024)(128)(2,1)}, u32[]{:S(2)}) copy-start(bf16[2048]{0:T(1024)(128)(2,1)} %param.11) | copy-start | bytes 12292
  165.7 11.0 %all-to-all-start.1 = ((f32[1,2,8,2,8]{4,3,1,0,2:T(2,128)}), f32[1,2,8,2,8]{4,3,1,0,2:T(2,128)S(1)}, u32[]{:S(2)}, u32[]{:S(2)}) async-start(f32[1,2,8,2,8]{4,3,1,0,2:T(2,128)} %copy.44), calls=%async_computation.1 | async-start | bytes 32768 | tf_op jit(solution)/shard_map/all_to_all | solution.py:100
  176.6 9.9 %all-to-all-start.3 = ((f32[1,2,8,2,8]{4,3,1,0,2:T(2,128)}), f32[1,2,8,2,8]{4,3,1,0,2:T(2,128)S(1)}, u32[]{:S(2)}, u32[]{:S(2)}) async-start(f32[1,2,8,2,8]{4,3,1,0,2:T(2,128)} %copy.52), calls=%async_computation.3 | async-start | bytes 32768 | tf_op jit(solution)/shard_map/all_to_all | solution.py:103
  186.5 10.7 %all-to-all-start.2 = ((f32[1,2,8,2,8,128]{5,4,3,1,0,2:T(8,128)}), f32[1,2,8,2,8,128]{5,4,3,1,0,2:T(8,128)S(1)}, u32[]{:S(2)}, u32[]{:S(2)}) async-start(f32[1,2,8,2,8,128]{5,4,3,1,0,2:T(8,128)} %copy.49), calls=%async_computation.2 | async-start | bytes 262144 | tf_op jit(solution)/shard_map/all_to_all | solution.py:106
Sparse Core Ops, SparseCore 0:
  96.3 67.3 all-reduce.1
where the time goes:
time: 206 us; the launch traced here: 205 us
  waiting for transfers between devices  90.1 us (44%)
  other arithmetic  46.9 us (23%)
  local copies, waits for them, and re-layouts  31 us (15%)
  starting transfers between devices  18.4 us (9%)
  between operations  14.3 us (7%)
  matrix products  4.29 us (2%)
    psum x1, waiting for transfers between devices, shards(): lax.psum(jnp.dot(flat_rows, weights_all, preferred_element_type=jnp.float...  67.2 us
    unnamed x1, other arithmetic  45.3 us
    unnamed x18, local copies, waits for them, and re-layouts  19.2 us
    all_to_all x2, local copies, waits for them, and re-layouts, shards(): lax.all_to_all(hidden, 'ctx', split_axis=2, concat_axis=0, tiled=True)  8.11 us
    all_to_all x1, starting transfers between devices, shards(): lax.all_to_all(hidden, 'ctx', split_axis=2, concat_axis=0, tiled=True)  7.28 us
    all_to_all x1, waiting for transfers between devices, shards(): lax.all_to_all(closing_state[2].reshape(lead_shape + (HEAD_SIZE,)), 'ctx'...  7.2 us
    all_to_all x1, waiting for transfers between devices, shards(): lax.all_to_all(closing_state[1].reshape(lead_shape), 'ctx', split_axis=2,...  6.48 us
    all_to_all x1, waiting for transfers between devices, shards(): lax.all_to_all(hidden, 'ctx', split_axis=2, concat_axis=0, tiled=True)  4.69 us
  transfers between devices with their start and end apart: 5, of which 5 were waited for; matrix products, arithmetic and copies ran while one was open for 2% of the time, Pallas kernels for 0%

commit v1 on v0

--- a/solution.py
+++ b/solution.py
@@ -17,7 +17,10 @@
     query_group_width = q_width // k_width
     score_scale = HEAD_SIZE ** (-0.5)
     row_count = 2 * tok_dev
-    columns = lax.all_to_all(hidden, "ctx", split_axis=2, concat_axis=0, tiled=True)
+    columns = jnp.concatenate(
+        lax.all_to_all(jnp.stack(jnp.split(hidden, lax.axis_size("ctx"), axis=2)), "ctx", 0, 0),
+        axis=0,
+    )
     flat_rows = columns.reshape(2 * resp_tokens, columns.shape[2])
     weights_all = jnp.concatenate((wq, wkv[0], wkv[1]), axis=1)
     bias_all = jnp.concatenate((bias_q, bias_kv[0], bias_kv[1])).astype(jnp.float32)

time: 206 us -> 146 us (0.71)
  other arithmetic: 46.9 us -> 2.88 us
  local copies, waits for them, and re-layouts: 31 us -> 16.2 us
    unnamed x1 -> x0, other arithmetic: 45.3 us -> none
    unnamed x18 -> x14, local copies, waits for them, and re-layouts: 19.2 us -> 9.29 us
    all_to_all x2 -> x0, local copies, waits for them, and re-layouts: 8.11 us -> none  [shards(): lax.all_to_all(hidden, 'ctx', split_axis=2, concat_axis=0, tiled=True)]
    all_to_all x1, waiting for transfers between devices: 4.69 us -> 1.46 us  [shards(): lax.all_to_all(jnp.stack(jnp.split(hidden, lax.axis_size('ctx'), axis=2))...]
    psum x1, waiting for transfers between devices: 67.2 us -> 69.7 us  [shards(): lax.psum(jnp.dot(flat_rows, weights_all, preferred_element_type=jnp.float...]
  transfers between devices with their start and end apart: 5 -> 5, of which waited for: 5 -> 5; matrix products, arithmetic and copies ran while one was open for 2% -> 5% of each run, Pallas kernels for 0% -> 0%
where the time goes in v1:
time: 146 us
  waiting for transfers between devices  89.4 us (61%)
  starting transfers between devices  18.4 us (13%)
  local copies, waits for them, and re-layouts  16.2 us (11%)
  between operations  14.2 us (10%)
  matrix products  4.29 us (3%)
  other arithmetic  2.88 us (2%)
    psum x1, waiting for transfers between devices, shards(): lax.psum(jnp.dot(flat_rows, weights_all, preferred_element_type=jnp.float...  69.7 us
    unnamed x14, local copies, waits for them, and re-layouts  9.29 us
    all_to_all x1, starting transfers between devices, shards(): lax.all_to_all(jnp.stack(jnp.split(hidden, lax.axis_size('ctx'), axis=2))...  7.28 us
    all_to_all x1, waiting for transfers between devices, shards(): lax.all_to_all(closing_state[2].reshape(lead_shape + (HEAD_SIZE,)), 'ctx'...  7.2 us
    all_to_all x1, waiting for transfers between devices, shards(): lax.all_to_all(closing_state[1].reshape(lead_shape), 'ctx', split_axis=2,...  6.48 us
    all_to_all x1, waiting for transfers between devices, shards(): lax.all_to_all(closing_state[0].reshape(lead_shape), 'ctx', split_axis=2,...  4.54 us
    all_to_all x1, starting transfers between devices, shards(): lax.all_to_all(closing_state[0].reshape(lead_shape), 'ctx', split_axis=2,...  4.4 us
    all_to_all x1, starting transfers between devices, shards(): lax.all_to_all(closing_state[2].reshape(lead_shape + (HEAD_SIZE,)), 'ctx'...  3.37 us
  transfers between devices with their start and end apart: 5, of which 5 were waited for; matrix products, arithmetic and copies ran while one was open for 5% of the time, Pallas kernels for 0%

profile of v1, /device:TPU:0, one launch (start us, length us, event | category | flops | bytes accessed | tf_op | source)
XLA Modules:
  0.0 145.5 jit_solution(17197644539874577633)
XLA Ops:
  6.5 1.3 constant_dynamic-update-slice_fusion.7
  7.8 1.3 constant_dynamic-update-slice_fusion.6
  9.1 1.3 constant_dynamic-update-slice_fusion.5
  10.4 1.3 constant_dynamic-update-slice_fusion.4
  11.7 1.3 constant_dynamic-update-slice_fusion.3
  12.9 1.3 constant_dynamic-update-slice_fusion.2
  14.2 1.3 constant_dynamic-update-slice_fusion.1
  15.5 1.3 constant_dynamic-update-slice_fusion
  16.8 7.3 %all-to-all-start = ((bf16[8,1,2,1024]{3,2,1,0:T(2,128)(2,1)}), bf16[8,1,2,1024]{3,2,1,0:T(2,128)(2,1)S(1)}, u32[]{:S(2)}, u32[]{:S(2)}) async-start(bf16[8,1,2,1024]{3,2,1,0:T(2,128)(2,1)} %constant_dynamic-update-slice_fusion), calls=%async_computation | async-start | bytes 65536 | tf_op jit(solution)/shard_map/all_to_all | solution.py:21
  24.1 0.0 all-reduce.2.cloned.1.call-start
  24.1 1.3 slice_bitcast_fusion.1
  25.4 0.7 broadcast_compare_fusion
  26.1 0.7 compare_and_fusion
  27.4 1.1 fusion.42
  28.5 0.8 slice_reduce_fusion.1
  29.3 1.5 %all-to-all-done = bf16[8,1,2,1024]{3,2,1,0:T(2,128)(2,1)S(1)} async-done(((bf16[8,1,2,1024]{3,2,1,0:T(2,128)(2,1)}), bf16[8,1,2,1024]{3,2,1,0:T(2,128)(2,1)S(1)}, u32[]{:S(2)}, u32[]{:S(2)}) %all-to-all-start) | async-done | bytes 32800 | tf_op jit(solution)/shard_map/all_to_all | solution.py:21
  30.8 0.0 copy-start
  30.8 3.3 %fusion = f32[16,2560]{1,0:T(8,128)} fusion(bf16[16,1024]{1,0:T(8,128)(2,1)S(1)} %reshape_reshape.3, bf16[1024,256]{1,0:T(8,128)(2,1)S(1)} %get-tuple-element.26, bf16[1024,256]{1,0:T(8,128)(2,1)S(1)} %get-tuple-element.25, bf16[1024,2048]{1,0:T(8,128)(2,1)} %param.9), kind=kOutput, calls=%fused_computation | convolution fusion | flops 99614720 | bytes 5439488 | tf_op jit(solution)/shard_map/dot_general | solution.py:27
  34.1 0.0 all-reduce.2.cloned.1.call-update
  34.2 0.1 copy.55
  34.3 0.1 copy.56
  34.5 0.0 copy-done
  34.5 69.7 %all-reduce.2.cloned.1.call-done = f32[16,2560]{1,0:T(8,128)} async-done(((f32[16,2560]{1,0:T(8,128)}), f32[16,2560]{1,0:T(8,128)}) %all-reduce.2.cloned.1.call-update) | async-done | bytes 163856 | tf_op jit(solution)/shard_map/psum | solution.py:27
  104.2 0.9 add_convert_fusion
  105.3 0.3 fusion.44
  105.6 0.6 copy.38
  106.2 4.4 %all-to-all-start.1 = ((f32[1,2,8,2,8]{4,3,1,0,2:T(2,128)}), f32[1,2,8,2,8]{4,3,1,0,2:T(2,128)S(1)}, u32[]{:S(2)}, u32[]{:S(2)}) async-start(f32[1,2,8,2,8]{4,3,1,0,2:T(2,128)} %copy.38), calls=%async_computation.1 | async-start | bytes 32768 | tf_op jit(solution)/shard_map/all_to_all | solution.py:103
  110.6 0.2 fusion.15
  110.8 0.3 convolution_add_fusion
  111.1 0.1 fusion.45
  111.3 0.1 fusion.26
  111.3 0.6 copy.46
  112.0 0.6 copy.43
  112.6 4.5 %all-to-all-done.1 = f32[1,2,8,2,8]{4,3,1,0,2:T(2,128)S(1)} async-done(((f32[1,2,8,2,8]{4,3,1,0,2:T(2,128)}), f32[1,2,8,2,8]{4,3,1,0,2:T(2,128)S(1)}, u32[]{:S(2)}, u32[]{:S(2)}) %all-to-all-start.1) | async-done | bytes 1056 | tf_op jit(solution)/shard_map/all_to_all | solution.py:103
  117.2 3.3 %all-to-all-start.3 = ((f32[1,2,8,2,8]{4,3,1,0,2:T(2,128)}), f32[1,2,8,2,8]{4,3,1,0,2:T(2,128)S(1)}, u32[]{:S(2)}, u32[]{:S(2)}) async-start(f32[1,2,8,2,8]{4,3,1,0,2:T(2,128)} %copy.46), calls=%async_computation.3 | async-start | bytes 32768 | tf_op jit(solution)/shard_map/all_to_all | solution.py:106
  120.5 6.5 %all-to-all-done.3 = f32[1,2,8,2,8]{4,3,1,0,2:T(2,128)S(1)} async-done(((f32[1,2,8,2,8]{4,3,1,0,2:T(2,128)}), f32[1,2,8,2,8]{4,3,1,0,2:T(2,128)S(1)}, u32[]{:S(2)}, u32[]{:S(2)}) %all-to-all-start.3) | async-done | bytes 1056 | tf_op jit(solution)/shard_map/all_to_all | solution.py:106
  127.0 3.4 %all-to-all-start.2 = ((f32[1,2,8,2,8,128]{5,4,3,1,0,2:T(8,128)}), f32[1,2,8,2,8,128]{5,4,3,1,0,2:T(8,128)S(1)}, u32[]{:S(2)}, u32[]{:S(2)}) async-start(f32[1,2,8,2,8,128]{5,4,3,1,0,2:T(8,128)} %copy.43), calls=%async_computation.2 | async-start | bytes 262144 | tf_op jit(solution)/shard_map/all_to_all | solution.py:109
  130.5 7.2 %all-to-all-done.2 = f32[1,2,8,2,8,128]{5,4,3,1,0,2:T(8,128)S(1)} async-done(((f32[1,2,8,2,8,128]{5,4,3,1,0,2:T(8,128)}), f32[1,2,8,2,8,128]{5,4,3,1,0,2:T(8,128)S(1)}, u32[]{:S(2)}, u32[]{:S(2)}) %all-to-all-start.2) | async-done | bytes 131104 | tf_op jit(solution)/shard_map/all_to_all | solution.py:109
  137.7 0.1 fusion.21
  137.8 0.2 fusion.12
  138.0 0.6 convert_element_type.36
  (18 shorter events, 0.2 us)
Async XLA Ops:
  16.8 14.0 %all-to-all-start = ((bf16[8,1,2,1024]{3,2,1,0:T(2,128)(2,1)}), bf16[8,1,2,1024]{3,2,1,0:T(2,128)(2,1)S(1)}, u32[]{:S(2)}, u32[]{:S(2)}) async-start(bf16[8,1,2,1024]{3,2,1,0:T(2,128)(2,1)} %constant_dynamic-update-slice_fusion), calls=%async_computation | async-start | bytes 65536 | tf_op jit(solution)/shard_map/all_to_all | solution.py:21
  24.1 80.2 %all-reduce.2.cloned.1.call-start = ((), (), s32[]{:S(2)}) async-start(), calls=%async_computation.4 | async-start | bytes 327680 | tf_op jit(solution)/shard_map/psum | solution.py:27
  30.8 3.7 %copy-start = (bf16[2048]{0:T(1024)(128)(2,1)S(1)}, bf16[2048]{0:T(1024)(128)(2,1)}, u32[]{:S(2)}) copy-start(bf16[2048]{0:T(1024)(128)(2,1)} %param.11) | copy-start | bytes 12292
  106.2 11.0 %all-to-all-start.1 = ((f32[1,2,8,2,8]{4,3,1,0,2:T(2,128)}), f32[1,2,8,2,8]{4,3,1,0,2:T(2,128)S(1)}, u32[]{:S(2)}, u32[]{:S(2)}) async-start(f32[1,2,8,2,8]{4,3,1,0,2:T(2,128)} %copy.38), calls=%async_computation.1 | async-start | bytes 32768 | tf_op jit(solution)/shard_map/all_to_all | solution.py:103
  117.2 9.9 %all-to-all-start.3 = ((f32[1,2,8,2,8]{4,3,1,0,2:T(2,128)}), f32[1,2,8,2,8]{4,3,1,0,2:T(2,128)S(1)}, u32[]{:S(2)}, u32[]{:S(2)}) async-start(f32[1,2,8,2,8]{4,3,1,0,2:T(2,128)} %copy.46), calls=%async_computation.3 | async-start | bytes 32768 | tf_op jit(solution)/shard_map/all_to_all | solution.py:106
  127.0 10.7 %all-to-all-start.2 = ((f32[1,2,8,2,8,128]{5,4,3,1,0,2:T(8,128)}), f32[1,2,8,2,8,128]{5,4,3,1,0,2:T(8,128)S(1)}, u32[]{:S(2)}, u32[]{:S(2)}) async-start(f32[1,2,8,2,8,128]{5,4,3,1,0,2:T(8,128)} %copy.43), calls=%async_computation.2 | async-start | bytes 262144 | tf_op jit(solution)/shard_map/all_to_all | solution.py:109
Sparse Core Ops, SparseCore 0:
  34.3 69.9 all-reduce.1
